TPU v7x, 32 devices: a whole 2x2x4 slice. The times are simulated.
32 devices in a mesh: prompts: 4 (over y, core), units: 8 (over z, x).
Axes of the slice: x: 2, y: 2, z: 4, core: 2. Of those that a mesh axis runs over, the one named last changes fastest.
Arguments:
- hidden_acts: bfloat16 [16, 2048, 14336], P('prompts', None, 'units'), may hold values from -6 to 6
- out_grads: bfloat16 [16, 2048, 4096], P('prompts', None, 'units'), may hold values from -6 to 6
- proj_in: bfloat16 [14336, 64], P('units'), may hold values from -0.29231698 to 0.29231698
- proj_out: bfloat16 [4096, 64], P('units'), may hold values from -0.09375 to 0.09375
- lengths: int32 [16], P('prompts'), may hold values from 256 to 2048
- val_grads: float32 [256, 4096], P('prompts', 'units'), may hold values from -6 to 6
Outputs:
- scores: float32 [16, 256], P('prompts')
All inputs are finite; a program needn't handle non-finite values.
Results may differ from a plain program's by a relative error of at most 0.0003.
Values sent between devices are 32-bit elements; how exact they have to be, the bound alone decides.
A program may use at most 128 MiB of HBM per device.

v0:
```python
import jax
import jax.numpy as jnp
from jax import lax
from jax.sharding import PartitionSpec as P


def project_rows(flat_acts, flat_grads, proj_in, proj_out):
    inner = jnp.dot(flat_acts, proj_in, preferred_element_type=jnp.float32)
    outer = jnp.dot(flat_grads, proj_out, preferred_element_type=jnp.float32)
    return jnp.concatenate([inner, outer], axis=1)


def per_device(hidden_acts, out_grads, proj_in, proj_out, lengths, val_grads):
    prompts_here, seq_len, units_here = hidden_acts.shape
    rank = proj_in.shape[1]
    total_rows = prompts_here * seq_len
    flat_acts = hidden_acts.reshape(total_rows, units_here)
    flat_grads = out_grads.reshape(total_rows, out_grads.shape[2])
    highest = lax.Precision.HIGHEST
    share = total_rows // lax.axis_size("units")
    summed = lax.psum_scatter(
        project_rows(flat_acts, flat_grads, proj_in, proj_out),
        "units",
        scatter_dimension=0,
        tiled=True,
    )
    row_ids = lax.axis_index("units") * share + jnp.arange(share, dtype=jnp.int32)
    prompt_of = row_ids // seq_len
    position = row_ids % seq_len
    onehot = (prompt_of[:, None] == jnp.arange(prompts_here, dtype=jnp.int32)[None, :]).astype(
        jnp.int32
    )
    length_of = jnp.sum(onehot * lengths[None, :], axis=1)
    valid = (position < length_of).astype(jnp.float32)
    weights = onehot.astype(jnp.float32) * valid[:, None]
    inner = summed[:, :rank]
    outer = summed[:, rank:]
    spread = (weights[:, :, None] * inner[:, None, :]).reshape(share, prompts_here * rank)
    partial_grads = jnp.einsum("rk,rj->kj", spread, outer, precision=highest).reshape(
        prompts_here, rank * rank
    )
    feature_grads = lax.psum_scatter(partial_grads, "units", scatter_dimension=1, tiled=True)
    val_local = lax.all_gather(val_grads, "prompts", axis=0, tiled=True)
    part_dots = jnp.einsum("pf,vf->pv", feature_grads, val_local, precision=highest)
    part_squares = jnp.sum(feature_grads * feature_grads, axis=1)
    dots, squares = lax.psum((part_dots, part_squares), "units")
    return dots / jnp.sqrt(squares + 1e-06)[:, None]


def solution(mesh):
    in_specs = (
        P("prompts", None, "units"),
        P("prompts", None, "units"),
        P("units", None),
        P("units", None),
        P("prompts"),
        P("prompts", "units"),
    )
    out_specs = P("prompts", None)
    return jax.shard_map(
        per_device, mesh=mesh, in_specs=in_specs, out_specs=out_specs, check_vma=False
    )
```

profile of v0, /device:TPU:0, one launch (start us, length us, event | category | flops | bytes accessed | tf_op | source)
XLA Modules:
  0.0 221.7 jit_solution(1714008461043155932)
XLA Ops:
  6.5 0.0 copy-start
  6.5 0.0 reduce-scatter.5.cloned.1.call-start
  6.5 0.9 copy-done
  7.5 0.0 copy-start.1
  7.5 0.0 copy-start.3
  7.5 14.3 %fusion.11 = f32[8192,64]{0,1:T(8,128)S(1)} fusion(bf16[8192,1792]{1,0:T(8,128)(2,1)} %bitcast.13, bf16[1792,64]{0,1:T(8,128)(2,1)S(1)} %copy-done), kind=kOutput, calls=%fused_computation.26 | convolution fusion | flops 1879048192 | bytes 31686656 | tf_op jit(solution)/shard_map/dot_general | solution.py:8
  21.8 0.0 copy-done.1
  21.8 0.0 copy-done.3
  21.8 2.6 %fusion.12 = f32[8192,64]{0,1:T(8,128)S(1)} fusion(bf16[8192,512]{1,0:T(8,128)(2,1)S(1)} %bitcast.14, bf16[512,64]{0,1:T(8,128)(2,1)S(1)} %copy-done.3), kind=kOutput, calls=%fused_computation.27 | convolution fusion | flops 536870912 | bytes 10551296 | tf_op jit(solution)/shard_map/dot_general | solution.py:9
  24.5 2.3 %pad_maximum_fusion = f32[8192,128]{0,1:T(8,128)} fusion(f32[8192,64]{0,1:T(8,128)S(1)} %fusion.12, f32[8192,64]{0,1:T(8,128)S(1)} %fusion.11), kind=kLoop, calls=%fused_computation | loop fusion | flops 1048576 | bytes 8388608 | tf_op jit(solution)/shard_map/concatenate | solution.py:10
  26.8 0.0 copy-start.4
  26.8 0.0 reduce-scatter.5.cloned.1.call-update
  26.8 0.0 copy-start.2
  26.8 0.0 reduce-scatter.7.cloned.1.call-start
  26.9 0.5 copy-done.4
  27.5 0.1 select_reduce_fusion
  27.6 90.8 %reduce-scatter.5.cloned.1.call-done = f32[1024,128]{0,1:T(8,128)} async-done(((f32[8192,128]{0,1:T(8,128)}), f32[1024,128]{0,1:T(8,128)}) %reduce-scatter.5.cloned.1.call-update) | async-done | bytes 524304 | tf_op jit(solution)/shard_map/reduce_scatter | solution.py:21
  118.4 1.0 slice.8
  119.4 0.1 broadcast_multiply_fusion
  119.5 1.9 fusion
  121.4 0.1 reshape.91
  121.5 2.0 copy.11
  123.5 0.0 reduce-scatter.7.cloned.1.call-update
  123.5 0.0 copy-done.2
  123.6 7.2 %all_gather.3 = f32[256,512]{1,0:T(8,128)S(1)} all-gather(f32[64,512]{1,0:T(8,128)S(1)} %copy-done.2), channel_id=1, replica_groups=mesh['prompts'=4,'units'=8] {'prompts'}, dimensions={0}, use_global_device_ids=true | all-gather | bytes 655360 | tf_op jit(solution)/shard_map/all_gather | solution.py:43
  130.7 61.4 %reduce-scatter.7.cloned.1.call-done = f32[512,4]{1,0:T(8,128)} async-done(((f32[4096,4]{1,0:T(8,128)}), f32[512,4]{1,0:T(8,128)}) %reduce-scatter.7.cloned.1.call-update) | async-done | bytes 8208
  192.1 1.1 copy.12
  193.2 0.1 multiply_reduce_fusion
  193.3 1.5 fusion.9
  194.8 19.4 %all-reduce = (f32[4,256]{1,0:T(4,128)S(1)}, f32[4]{0:T(128)S(1)}) all-reduce(f32[4,256]{1,0:T(4,128)S(1)} %fusion.9, f32[4]{0:T(128)S(1)} %multiply_reduce_fusion), channel_id=1, replica_groups=mesh['prompts'=4,'units'=8] {'units'}, use_global_device_ids=true, to_apply=%region_3.4 | all-reduce | flops 1028 | bytes 8224 | tf_op jit(solution)/shard_map/psum | solution.py:46
  214.2 0.7 broadcast_divide_fusion
  (4 shorter events, 0.0 us)
Async XLA Ops:
  6.5 0.9 copy-start
  6.5 111.9 %reduce-scatter.5.cloned.1.call-start = ((), (), s32[]{:S(2)}) async-start(), calls=%async_computation.2 | async-start | bytes 4718592 | tf_op jit(solution)/shard_map/reduce_scatter | solution.py:21
  7.5 14.4 %copy-start.1 = (bf16[4,2048,512]{2,1,0:T(8,128)(2,1)S(1)}, bf16[4,2048,512]{2,1,0:T(8,128)(2,1)}, u32[]{:S(2)}) copy-start(bf16[4,2048,512]{2,1,0:T(8,128)(2,1)} %param.7) | copy-start | bytes 25165828
  7.5 14.4 %copy-start.3 = (bf16[512,64]{0,1:T(8,128)(2,1)S(1)}, bf16[512,64]{0,1:T(8,128)(2,1)}, u32[]{:S(2)}) copy-start(bf16[512,64]{0,1:T(8,128)(2,1)} %param.9) | copy-start | bytes 196612
  26.8 0.7 copy-start.4
  26.8 96.7 %copy-start.2 = (f32[64,512]{1,0:T(8,128)S(1)}, f32[64,512]{1,0:T(8,128)}, u32[]{:S(2)}) copy-start(f32[64,512]{1,0:T(8,128)} %param.11) | copy-start | bytes 393220
  26.8 165.3 %reduce-scatter.7.cloned.1.call-start = ((), (), s32[]{:S(2)}) async-start(), calls=%async_computation.3 | async-start | bytes 2359296
Sparse Core Ops, SparseCore 0:
  26.9 91.4 reduce-scatter.4
  123.7 68.4 reduce-scatter.6
where the time goes:
time: 222 us
  waiting for transfers between devices  152 us (68%)
  blocking collectives  26.5 us (12%)
  matrix products  20.4 us (9%)
  between operations  13.5 us (6%)
  local copies, waits for them, and re-layouts  5.63 us (3%)
  other arithmetic  3.35 us (2%)
    reduce_scatter x1, waiting for transfers between devices, per_device(): lax.psum_scatter(project_rows(flat_acts, flat_grads, proj_in, proj_out),...  90.8 us
    unnamed x3, waiting for transfers between devices  61.5 us
    psum x1, blocking collectives, per_device(): dots, squares = lax.psum((part_dots, part_squares), 'units')  19.4 us
    dot_general x1, matrix products, project_rows(): inner = jnp.dot(flat_acts, proj_in, preferred_element_type=jnp.float32)  14.3 us
    all_gather x1, blocking collectives, per_device(): val_local = lax.all_gather(val_grads, 'prompts', axis=0, tiled=True)  7.16 us
    unnamed x12, local copies, waits for them, and re-layouts  4.55 us
  transfers between devices with their start and end apart: 2, of which 2 were waited for; matrix products, arithmetic and copies ran while one was open for 0% of the time, Pallas kernels for 0%

commit v1 on v0

v1 whole, which is shorter than its diff:
```python
import functools
import math

import jax
import jax.numpy as jnp
from jax import lax
from jax.experimental import pallas as pl
from jax.experimental.pallas import tpu as pltpu
from jax.sharding import PartitionSpec as P

MESH = pl.DeviceIdType.MESH
HIGHEST = lax.Precision.HIGHEST
LANES = 128
SUB = 128


def kernel(
    cfg,
    acts, grads, win, wout, lens, val,
    out,
    abuf, gbuf, wi, wo, sx, own, rx, pre, suf, psend, ssend, macc, gsend, grecv, vall, dsend, drecv,
    hbm_sem, x_s, x_r, pre_s, pre_r, suf_s, suf_r, v_s, v_r, v_l, g_s, g_r, d_s, d_r,
):
    N, I, O, Q = cfg["N"], cfg["I"], cfg["O"], cfg["Q"]
    ct, ncb, nb, spc = cfg["ct"], cfg["ncb"], cfg["nb"], cfg["spc"]
    seq, p_here, p_own, rank = cfg["seq"], cfg["p_here"], cfg["p_own"], cfg["rank"]
    rows_own = ncb * ct
    half = ct // 2
    K = I * ncb
    me = lax.axis_index("units")
    q = lax.axis_index("prompts")
    o = me // I
    i = me % I

    barrier = pltpu.get_barrier_semaphore()
    for d in range(1, N):
        pl.semaphore_signal(barrier, inc=1, device_id={"units": (me + d) % N}, device_id_type=MESH)
    for d in range(1, Q):
        pl.semaphore_signal(barrier, inc=1, device_id={"prompts": (q + d) % Q}, device_id_type=MESH)

    def fetch(k):
        owner = (i + 1 + k // ncb) % I
        row0 = pl.multiple_of(owner * rows_own + (k % ncb) * ct, ct)
        slot = k % 2
        return (
            pltpu.make_async_copy(acts.at[pl.ds(row0, ct)], abuf.at[slot], hbm_sem.at[slot, 0]),
            pltpu.make_async_copy(grads.at[pl.ds(row0, ct)], gbuf.at[slot], hbm_sem.at[slot, 1]),
        )

    for copy in fetch(0):
        copy.start()

    zero_i = jnp.zeros(win.shape, win.dtype)
    wi[0] = jnp.concatenate([win[...], zero_i], axis=1)
    wi[1] = jnp.concatenate([zero_i, win[...]], axis=1)
    zero_o = jnp.zeros(wout.shape, wout.dtype)
    wo[0] = jnp.concatenate([wout[...], zero_o], axis=1)
    wo[1] = jnp.concatenate([zero_o, wout[...]], axis=1)
    macc[...] = jnp.zeros_like(macc)

    vrows = val.shape[0]
    mine = vall.at[pl.ds(pl.multiple_of(q * vrows, vrows), vrows)]
    val_own = pltpu.make_async_copy(val, mine, v_l)
    val_own.start()

    pl.semaphore_wait(barrier, N - 1 + Q - 1)

    def val_copy(d):
        return pltpu.make_async_remote_copy(
            src_ref=val, dst_ref=mine, send_sem=v_s.at[d - 1], recv_sem=v_r.at[d - 1],
            device_id={"prompts": (q + d) % Q}, device_id_type=MESH,
        )

    for d in range(1, Q):
        val_copy(d).start()

    def project(k, store):
        @pl.when(k + 1 < K)
        def _():
            for copy in fetch(k + 1):
                copy.start()

        for copy in fetch(k):
            copy.wait()
        slot = k % 2
        for side, (buf, w) in enumerate(((abuf, wi), (gbuf, wo))):
            part = jnp.dot(buf[slot, :half], w[0], preferred_element_type=jnp.float32)
            part += jnp.dot(buf[slot, half:], w[1], preferred_element_type=jnp.float32)
            for s in range(spc):
                store(s, side, part[s * SUB : (s + 1) * SUB])

    def x_copy(e, b):
        return pltpu.make_async_remote_copy(
            src_ref=sx.at[e, b], dst_ref=rx.at[e, b], send_sem=x_s.at[e, b], recv_sem=x_r.at[e, b],
            device_id={"units": o * I + (i + 1 + e) % I}, device_id_type=MESH,
        )

    def first(k, carry):
        e = k // ncb
        base = (k % ncb) * spc

        def store(s, side, x):
            sx[e, base + s, side] = x

        project(k, store)
        for s in range(spc):
            x_copy(e, base + s).start()
        return carry

    lax.fori_loop(0, (I - 1) * ncb, first, 0)

    def second(c, carry):
        def store(s, side, x):
            own[c * spc + s, side] = x

        project((I - 1) * ncb + c, store)
        return carry

    lax.fori_loop(0, ncb, second, 0)

    def right_copy(b):
        return pltpu.make_async_remote_copy(
            src_ref=psend.at[b], dst_ref=pre.at[b], send_sem=pre_s.at[b], recv_sem=pre_r.at[b],
            device_id={"units": (me + I) % N}, device_id_type=MESH,
        )

    def left_copy(b):
        return pltpu.make_async_remote_copy(
            src_ref=ssend.at[b], dst_ref=suf.at[b], send_sem=suf_s.at[b], recv_sem=suf_r.at[b],
            device_id={"units": (me + N - I) % N}, device_id_type=MESH,
        )

    def third(t, carry):
        @pl.when(t < nb)
        def _():
            for e in range(I - 1):
                x_copy(e, t).wait_recv()
            a = own[t, 0]
            g = own[t, 1]
            for e in range(I - 1):
                a += rx[e, t, 0]
                g += rx[e, t, 1]
            own[t, 0] = a
            tok0 = (t // spc) * ct
            pos = tok0 % seq + (t % spc) * SUB + lax.broadcasted_iota(jnp.int32, (SUB, LANES), 0)
            lane = lax.broadcasted_iota(jnp.int32, (SUB, LANES), 1)
            pos = pos + jnp.where(lane < rank, 0, half)
            length = lens[i * p_own + tok0 // seq]
            own[t, 1] = jnp.where(pos < length, g, 0.0)

        br = t - o

        @pl.when((br >= 0) & (br < nb))
        def _():
            @pl.when(o == 0)
            def _():
                psend[br] = own[br, 0]

            @pl.when(o > 0)
            def _():
                right_copy(br).wait_recv()
                psend[br] = own[br, 0] + pre[br]

            @pl.when(o < O - 1)
            def _():
                right_copy(br).start()

        bl = t - (O - 1 - o)

        @pl.when((bl >= 0) & (bl < nb))
        def _():
            @pl.when(o == O - 1)
            def _():
                ssend[bl] = own[bl, 0]

            @pl.when(o < O - 1)
            def _():
                left_copy(bl).wait_recv()
                ssend[bl] = own[bl, 0] + suf[bl]

            @pl.when(o > 0)
            def _():
                left_copy(bl).start()

        b = t - (O - 1)

        @pl.when(b >= 0)
        def _():
            def add(x):
                p = ((b // spc) * ct) // seq
                macc[p] += lax.dot_general(
                    x, own[b, 1], (((0,), (0,)), ((), ())), precision=HIGHEST,
                    preferred_element_type=jnp.float32,
                )

            @pl.when(o < O - 1)
            def _():
                add(psend[b] + suf[b])

            @pl.when(o == O - 1)
            def _():
                add(psend[b])

        return carry

    lax.fori_loop(0, nb + O - 1, third, 0)

    grows = gsend.shape[2]
    for p in range(p_own):
        m = macc[p]
        g = m[:rank, :rank] + m[rank:, rank:]
        g2 = jnp.concatenate([g, g], axis=1)
        for n in range(N):
            gsend[n, p] = g2[n * grows : (n + 1) * grows]

    def g_copy(d):
        to = (me + d) % N
        return pltpu.make_async_remote_copy(
            src_ref=gsend.at[to], dst_ref=grecv.at[me], send_sem=g_s.at[d - 1], recv_sem=g_r.at[d - 1],
            device_id={"units": to}, device_id_type=MESH,
        )

    for d in range(1, N):
        g_copy(d).start()
    grecv[me] = gsend[me]
    val_own.wait()
    for d in range(1, Q):
        val_copy(d).wait()
    for d in range(1, N):
        g_copy(d).wait()

    lane = lax.broadcasted_iota(jnp.int32, (1, LANES), 1)
    rows = []
    for p in range(p_here):
        x, k = p // p_own, p % p_own
        s = grecv[x, k]
        for z in range(1, O):
            s += grecv[z * I + x, k]
        flat = [
            jnp.where(lane < rank, s[2 * r : 2 * r + 1], s[2 * r + 1 : 2 * r + 2])
            for r in range(grows // 2)
        ]
        rows.append(jnp.concatenate(flat, axis=1))
    pad = dsend.shape[0] - p_here
    feat = jnp.concatenate(rows + [jnp.zeros((pad, rows[0].shape[1]), jnp.float32)], axis=0)
    nval = vall.shape[0]
    dsend[:, :nval] = lax.dot_general(
        feat, vall[...], (((1,), (1,)), ((), ())), precision=HIGHEST,
        preferred_element_type=jnp.float32,
    )
    dsend[:, nval:] = jnp.broadcast_to(
        jnp.sum(feat * feat, axis=1, keepdims=True), (dsend.shape[0], LANES)
    )

    def d_copy(d):
        return pltpu.make_async_remote_copy(
            src_ref=dsend, dst_ref=drecv.at[me], send_sem=d_s.at[d - 1], recv_sem=d_r.at[d - 1],
            device_id={"units": (me + d) % N}, device_id_type=MESH,
        )

    for d in range(1, N):
        d_copy(d).start()
    drecv[me] = dsend[...]

    def drain(b, carry):
        for e in range(I - 1):
            x_copy(e, b).wait_send()

        @pl.when(o < O - 1)
        def _():
            right_copy(b).wait_send()

        @pl.when(o > 0)
        def _():
            left_copy(b).wait_send()

        return carry

    lax.fori_loop(0, nb, drain, 0)
    for d in range(1, N):
        d_copy(d).wait()
    total = drecv[0]
    for n in range(1, N):
        total += drecv[n]
    out[...] = total[:p_here, :nval] / jnp.sqrt(total[:p_here, nval : nval + 1] + 1e-06)


def per_device(inner, hidden_acts, out_grads, proj_in, proj_out, lengths, val_grads):
    p_here, seq, units_here = hidden_acts.shape
    rank = proj_in.shape[1]
    N, Q = lax.axis_size("units"), lax.axis_size("prompts")
    I = inner
    O = N // I
    p_own = p_here // I
    rows_own = p_own * seq
    ct = min(1024, seq)
    ncb = rows_own // ct
    spc = ct // 2 // SUB
    nb = ncb * spc
    feats = val_grads.shape[1]
    grows = feats // rank
    nval = val_grads.shape[0] * Q
    cfg = dict(
        N=N, I=I, O=O, Q=Q, ct=ct, ncb=ncb, nb=nb, spc=spc, seq=seq, p_here=p_here, p_own=p_own, rank=rank
    )
    f32 = jnp.float32
    dma = pltpu.SemaphoreType.DMA
    block = (SUB, LANES)
    drows = -(-p_here // 8) * 8
    vmem = pl.BlockSpec(memory_space=pltpu.VMEM)
    hbm = pl.BlockSpec(memory_space=pl.ANY)
    return pl.pallas_call(
        functools.partial(kernel, cfg),
        out_shape=jax.ShapeDtypeStruct((p_here, nval), f32),
        in_specs=[hbm, hbm, vmem, vmem, pl.BlockSpec(memory_space=pltpu.SMEM), vmem],
        out_specs=vmem,
        scratch_shapes=[
            pltpu.VMEM((2, ct, units_here), hidden_acts.dtype),
            pltpu.VMEM((2, ct, out_grads.shape[2]), out_grads.dtype),
            pltpu.VMEM((2, units_here, LANES), proj_in.dtype),
            pltpu.VMEM((2, out_grads.shape[2], LANES), proj_out.dtype),
            pltpu.VMEM((I - 1, nb, 2) + block, f32),
            pltpu.VMEM((nb, 2) + block, f32),
            pltpu.VMEM((I - 1, nb, 2) + block, f32),
            pltpu.VMEM((nb,) + block, f32),
            pltpu.VMEM((nb,) + block, f32),
            pltpu.VMEM((nb,) + block, f32),
            pltpu.VMEM((nb,) + block, f32),
            pltpu.VMEM((p_own, LANES, LANES), f32),
            pltpu.VMEM((N, p_own, grows, LANES), f32),
            pltpu.VMEM((N, p_own, grows, LANES), f32),
            pltpu.VMEM((nval, feats), f32),
            pltpu.VMEM((drows, nval + LANES), f32),
            pltpu.VMEM((N, drows, nval + LANES), f32),
            dma((2, 2)),
            dma((I - 1, nb)), dma((I - 1, nb)),
            dma((nb,)), dma((nb,)), dma((nb,)), dma((nb,)),
            dma((Q - 1,)), dma((Q - 1,)), dma,
            dma((N - 1,)), dma((N - 1,)), dma((N - 1,)), dma((N - 1,)),
        ],
        compiler_params=pltpu.CompilerParams(
            collective_id=0, has_side_effects=True, vmem_limit_bytes=60 * 1024 * 1024
        ),
    )(
        hidden_acts.reshape(p_here * seq, units_here),
        out_grads.reshape(p_here * seq, out_grads.shape[2]),
        proj_in, proj_out, lengths, val_grads,
    )


def solution(mesh):
    inner = 2 ** (int(math.log2(mesh.shape["units"])) // 2)
    in_specs = (
        P("prompts", None, "units"),
        P("prompts", None, "units"),
        P("units", None),
        P("units", None),
        P("prompts"),
        P("prompts", "units"),
    )
    return jax.shard_map(
        functools.partial(per_device, inner), mesh=mesh, in_specs=in_specs,
        out_specs=P("prompts", None), check_vma=False,
    )
```

time: 222 us -> 95.2 us (0.43)
  waiting for transfers between devices: 152 us -> 0 us
  Pallas kernels: 0 us -> 90.2 us
  blocking collectives: 26.5 us -> 0 us
  matrix products: 20.4 us -> 0 us
  between operations: 13.5 us -> 0.01 us
  other arithmetic: 3.35 us -> 0 us
    reduce_scatter x1 -> x0, waiting for transfers between devices: 90.8 us -> none  [per_device(): lax.psum_scatter(project_rows(flat_acts, flat_grads, proj_in, proj_out),...]
    pallas_call x0 -> x1, Pallas kernels: none -> 90.2 us  [per_device(): pl.pallas_call(functools.partial(kernel, cfg), out_shape=jax.ShapeDtypeSt...]
    unnamed x3 -> x0, waiting for transfers between devices: 61.5 us -> none
    dot_general x4 -> x0, matrix products: 20.4 us -> none  [the longest x1 14.3 us: project_rows(): inner = jnp.dot(flat_acts, proj_in, preferred_element_type=jnp.float32)]
    psum x1 -> x0, blocking collectives: 19.4 us -> none  [per_device(): dots, squares = lax.psum((part_dots, part_squares), 'units')]
    all_gather x1 -> x0, blocking collectives: 7.16 us -> none  [per_device(): val_local = lax.all_gather(val_grads, 'prompts', axis=0, tiled=True)]
    concatenate x1 -> x0, other arithmetic: 2.33 us -> none  [project_rows(): return jnp.concatenate([inner, outer], axis=1)]
    unnamed x12 -> x3, local copies, waits for them, and re-layouts: 4.55 us -> 4.79 us
  transfers between devices with their start and end apart: 2 -> 0, of which waited for: 2 -> 0; matrix products, arithmetic and copies ran while one was open for 0% -> 0% of each run, Pallas kernels for 0% -> 0%
where the time goes in v1:
time: 95.2 us; the launch traced here: 95 us
  Pallas kernels  90.2 us (95%)
  local copies, waits for them, and re-layouts  4.79 us (5%)
    pallas_call x1, Pallas kernels, per_device(): pl.pallas_call(functools.partial(kernel, cfg), out_shape=jax.ShapeDtypeSt...  90.2 us
    unnamed x3, local copies, waits for them, and re-layouts  4.79 us

profile of v1, /device:TPU:0, one launch (start us, length us, event | category | flops | bytes accessed | tf_op | source)
XLA Modules:
  0.0 95.0 jit_solution(18093268081047989715)
XLA Ops:
  0.0 1.6 %copy.8.wout = bf16[512,64]{1,0:T(8,128)(2,1)} copy(bf16[512,64]{0,1:T(8,128)(2,1)} %param.9) | data formatting | bytes 131072 | tf_op args[3]
  1.6 1.9 %copy.7.win = bf16[1792,64]{1,0:T(8,128)(2,1)} copy(bf16[1792,64]{0,1:T(8,128)(2,1)} %param.8) | data formatting | bytes 458752 | tf_op args[2]
  3.5 90.2 %shard_map.64 = f32[4,256]{1,0:T(4,128)} custom-call(bf16[8192,1792]{1,0:T(8,128)(2,1)} %bitcast.2, bf16[8192,512]{1,0:T(8,128)(2,1)} %bitcast.3, bf16[1792,64]{1,0:T(8,128)(2,1)} %copy.7.win, bf16[512,64]{1,0:T(8,128)(2,1)} %copy.8.wout, s32[4]{0:T(128)} %lens.1, f32[64,512]{1,0:T(8,128)} %val.1), custom_call_target="tpu_custom_call" | custom-call | tf_op jit(solution)/shard_map/pallas_call | solution.py:312
  93.7 1.3 %copy.10 = f32[4,256]{1,0:T(4,128)} copy(f32[4,256]{1,0:T(4,128)} %shard_map.64) | data formatting | bytes 8192

commit v2 on v1

--- a/solution.py
+++ b/solution.py
@@ -11,6 +11,7 @@
 MESH = pl.DeviceIdType.MESH
 HIGHEST = lax.Precision.HIGHEST
 LANES = 128
+SKEW = 2
 SUB = 128
 
 
@@ -50,12 +51,11 @@
     for copy in fetch(0):
         copy.start()
 
-    zero_i = jnp.zeros(win.shape, win.dtype)
-    wi[0] = jnp.concatenate([win[...], zero_i], axis=1)
-    wi[1] = jnp.concatenate([zero_i, win[...]], axis=1)
-    zero_o = jnp.zeros(wout.shape, wout.dtype)
-    wo[0] = jnp.concatenate([wout[...], zero_o], axis=1)
-    wo[1] = jnp.concatenate([zero_o, wout[...]], axis=1)
+    for w, dst in ((win, wi), (wout, wo)):
+        t = w[...].astype(jnp.float32)
+        zero = jnp.zeros_like(t)
+        dst[0] = jnp.concatenate([t, zero], axis=0).T.astype(dst.dtype)
+        dst[1] = jnp.concatenate([zero, t], axis=0).T.astype(dst.dtype)
     macc[...] = jnp.zeros_like(macc)
 
     vrows = val.shape[0]
@@ -63,16 +63,11 @@
     val_own = pltpu.make_async_copy(val, mine, v_l)
     val_own.start()
 
-    pl.semaphore_wait(barrier, N - 1 + Q - 1)
-
     def val_copy(d):
         return pltpu.make_async_remote_copy(
             src_ref=val, dst_ref=mine, send_sem=v_s.at[d - 1], recv_sem=v_r.at[d - 1],
             device_id={"prompts": (q + d) % Q}, device_id_type=MESH,
         )
-
-    for d in range(1, Q):
-        val_copy(d).start()
 
     def project(k, store):
         @pl.when(k + 1 < K)
@@ -95,19 +90,27 @@
             device_id={"units": o * I + (i + 1 + e) % I}, device_id_type=MESH,
         )
 
+    def first_compute(k):
+        def store(s, side, x):
+            sx[k // ncb, (k % ncb) * spc + s, side] = x
+
+        project(k, store)
+
+    def first_send(k):
+        for s in range(spc):
+            x_copy(k // ncb, (k % ncb) * spc + s).start()
+
     def first(k, carry):
-        e = k // ncb
-        base = (k % ncb) * spc
-
-        def store(s, side, x):
-            sx[e, base + s, side] = x
-
-        project(k, store)
-        for s in range(spc):
-            x_copy(e, base + s).start()
+        first_compute(k)
+        first_send(k)
         return carry
 
-    lax.fori_loop(0, (I - 1) * ncb, first, 0)
+    first_compute(0)
+    pl.semaphore_wait(barrier, N - 1 + Q - 1)
+    first_send(0)
+    for d in range(1, Q):
+        val_copy(d).start()
+    lax.fori_loop(1, (I - 1) * ncb, first, 0)
 
     def second(c, carry):
         def store(s, side, x):
@@ -148,7 +151,7 @@
             length = lens[i * p_own + tok0 // seq]
             own[t, 1] = jnp.where(pos < length, g, 0.0)
 
-        br = t - o
+        br = t - SKEW * o
 
         @pl.when((br >= 0) & (br < nb))
         def _():
@@ -165,7 +168,7 @@
             def _():
                 right_copy(br).start()
 
-        bl = t - (O - 1 - o)
+        bl = t - SKEW * (O - 1 - o)
 
         @pl.when((bl >= 0) & (bl < nb))
         def _():
@@ -182,7 +185,7 @@
             def _():
                 left_copy(bl).start()
 
-        b = t - (O - 1)
+        b = t - SKEW * (O - 1)
 
         @pl.when(b >= 0)
         def _():
@@ -203,7 +206,7 @@
 
         return carry
 
-    lax.fori_loop(0, nb + O - 1, third, 0)
+    lax.fori_loop(0, nb + SKEW * (O - 1), third, 0)
 
     grows = gsend.shape[2]
     for p in range(p_own):
@@ -344,7 +347,7 @@
     )(
         hidden_acts.reshape(p_here * seq, units_here),
         out_grads.reshape(p_here * seq, out_grads.shape[2]),
-        proj_in, proj_out, lengths, val_grads,
+        proj_in.T, proj_out.T, lengths, val_grads,
     )
 
 

time: 95.2 us -> 78.4 us (0.82)
  Pallas kernels: 90.2 us -> 76.9 us
  local copies, waits for them, and re-layouts: 4.79 us -> 1.28 us
    pallas_call x1, Pallas kernels: 90.2 us -> 76.9 us  [per_device(): pl.pallas_call(functools.partial(kernel, cfg), out_shape=jax.ShapeDtypeSt...]
    unnamed x3 -> x1, local copies, waits for them, and re-layouts: 4.79 us -> 1.28 us
where the time goes in v2:
time: 78.4 us; the launch traced here: 78.2 us
  Pallas kernels  76.9 us (98%)
  local copies, waits for them, and re-layouts  1.28 us (2%)
    pallas_call x1, Pallas kernels, per_device(): pl.pallas_call(functools.partial(kernel, cfg), out_shape=jax.ShapeDtypeSt...  76.9 us

profile of v2, /device:TPU:0, one launch (start us, length us, event | category | flops | bytes accessed | tf_op | source)
XLA Modules:
  0.0 78.2 jit_solution(7789382812512746770)
XLA Ops:
  0.0 76.9 %shard_map.64 = f32[4,256]{1,0:T(4,128)} custom-call(bf16[8192,1792]{1,0:T(8,128)(2,1)} %bitcast.4, bf16[8192,512]{1,0:T(8,128)(2,1)} %bitcast.5, bf16[64,1792]{1,0:T(8,128)(2,1)} %bitcast.6, bf16[64,512]{1,0:T(8,128)(2,1)} %bitcast.7, s32[4]{0:T(128)} %lens.1, f32[64,512]{1,0:T(8,128)} %val.1), custom_call_target="tpu_custom_call" | custom-call | tf_op jit(solution)/shard_map/pallas_call | solution.py:315
  76.9 1.3 %copy.8 = f32[4,256]{1,0:T(4,128)} copy(f32[4,256]{1,0:T(4,128)} %shard_map.64) | data formatting | bytes 8192

commit v3 on v2

--- a/solution.py
+++ b/solution.py
@@ -11,7 +11,10 @@
 MESH = pl.DeviceIdType.MESH
 HIGHEST = lax.Precision.HIGHEST
 LANES = 128
-SKEW = 2
+SKEW = 3
+EARLY = 3
+OWNAT = 2
+FIN = 0
 SUB = 128
 
 
@@ -20,14 +23,18 @@
     acts, grads, win, wout, lens, val,
     out,
     abuf, gbuf, wi, wo, sx, own, rx, pre, suf, psend, ssend, macc, gsend, grecv, vall, dsend, drecv,
-    hbm_sem, x_s, x_r, pre_s, pre_r, suf_s, suf_r, v_s, v_r, v_l, g_s, g_r, d_s, d_r,
+    t2, t2pre, t2suf, t2ps, t2ss, tt, rt, hbm_sem, x_s, x_r, pre_s, pre_r, suf_s, suf_r, v_s, v_r, v_l, g_s, g_r, d_s, d_r,
+    p2_s, p2_r, s2_s, s2_r, x2_s, x2_r,
 ):
     N, I, O, Q = cfg["N"], cfg["I"], cfg["O"], cfg["Q"]
     ct, ncb, nb, spc = cfg["ct"], cfg["ncb"], cfg["nb"], cfg["spc"]
-    seq, p_here, p_own, rank = cfg["seq"], cfg["p_here"], cfg["p_own"], cfg["rank"]
+    seq, p_here, rank = cfg["seq"], cfg["p_here"], cfg["rank"]
+    nc2, nb2 = cfg["nc2"], cfg["nb2"]
+    per = nb2 // O
     rows_own = ncb * ct
     half = ct // 2
-    K = I * ncb
+    K = I * ncb + nc2
+    OWN2 = min(nb2 + OWNAT, nb - 1)
     me = lax.axis_index("units")
     q = lax.axis_index("prompts")
     o = me // I
@@ -40,8 +47,12 @@
         pl.semaphore_signal(barrier, inc=1, device_id={"prompts": (q + d) % Q}, device_id_type=MESH)
 
     def fetch(k):
-        owner = (i + 1 + k // ncb) % I
-        row0 = pl.multiple_of(owner * rows_own + (k % ncb) * ct, ct)
+        if isinstance(k, int) and 1 <= k <= nc2:
+            row0 = I * rows_own + (k - 1) * ct
+        else:
+            kk = 0 if isinstance(k, int) and k == 0 else k - nc2
+            owner = (i + 1 + kk // ncb) % I
+            row0 = pl.multiple_of(owner * rows_own + (kk % ncb) * ct, ct)
         slot = k % 2
         return (
             pltpu.make_async_copy(acts.at[pl.ds(row0, ct)], abuf.at[slot], hbm_sem.at[slot, 0]),
@@ -70,10 +81,14 @@
         )
 
     def project(k, store):
-        @pl.when(k + 1 < K)
-        def _():
+        if isinstance(k, int):
             for copy in fetch(k + 1):
                 copy.start()
+        else:
+            @pl.when(k + 1 < K)
+            def _():
+                for copy in fetch(k + 1):
+                    copy.start()
 
         for copy in fetch(k):
             copy.wait()
@@ -90,9 +105,9 @@
             device_id={"units": o * I + (i + 1 + e) % I}, device_id_type=MESH,
         )
 
-    def first_compute(k):
+    def first_compute(k, kk):
         def store(s, side, x):
-            sx[k // ncb, (k % ncb) * spc + s, side] = x
+            sx[kk // ncb, (kk % ncb) * spc + s, side] = x
 
         project(k, store)
 
@@ -100,26 +115,118 @@
         for s in range(spc):
             x_copy(k // ncb, (k % ncb) * spc + s).start()
 
-    def first(k, carry):
-        first_compute(k)
-        first_send(k)
+    def first(kk, carry):
+        first_compute(kk + nc2, kk)
+        first_send(kk)
         return carry
 
-    first_compute(0)
+    first_compute(0, 0)
     pl.semaphore_wait(barrier, N - 1 + Q - 1)
     first_send(0)
     for d in range(1, Q):
         val_copy(d).start()
+
+    def right2(b, src):
+        return pltpu.make_async_remote_copy(
+            src_ref=src.at[b], dst_ref=t2pre.at[b], send_sem=p2_s.at[b], recv_sem=p2_r.at[b],
+            device_id={"units": (me + I) % N}, device_id_type=MESH,
+        )
+
+    def left2(b, src):
+        return pltpu.make_async_remote_copy(
+            src_ref=src.at[b], dst_ref=t2suf.at[b], send_sem=s2_s.at[b], recv_sem=s2_r.at[b],
+            device_id={"units": (me + N - I) % N}, device_id_type=MESH,
+        )
+
+    def x2_copy(e, n):
+        to = (i + 1 + e) % I
+        return pltpu.make_async_remote_copy(
+            src_ref=tt.at[to * (per // I) + n], dst_ref=rt.at[e, n],
+            send_sem=x2_s.at[e, n], recv_sem=x2_r.at[e, n],
+            device_id={"units": o * I + to}, device_id_type=MESH,
+        )
+
+    for c2 in range(nc2):
+        def store2(s, side, x, c2=c2):
+            t2[c2 * spc + s, side] = x
+
+        project(1 + c2, store2)
+
+    if nc2:
+        @pl.when(o == 0)
+        def _():
+            for b in range(nb2 - 1, max(per, nb2 - EARLY) - 1, -1):
+                right2(b, t2).start()
+
+        @pl.when(o == O - 1)
+        def _():
+            for b in range(min(nb2 - per, EARLY)):
+                left2(b, t2).start()
+
     lax.fori_loop(1, (I - 1) * ncb, first, 0)
 
     def second(c, carry):
         def store(s, side, x):
             own[c * spc + s, side] = x
 
-        project((I - 1) * ncb + c, store)
+        project(nc2 + (I - 1) * ncb + c, store)
         return carry
 
     lax.fori_loop(0, ncb, second, 0)
+
+    def relay2(t):
+        ir = t - SKEW * o
+        b = nb2 - 1 - ir
+        il = t - SKEW * (O - 1 - o)
+
+        @pl.when((o == 0) & (ir >= EARLY) & (ir < nb2 - per))
+        def _():
+            right2(b, t2).start()
+
+        @pl.when((o > 0) & (ir >= 0) & (ir < nb2 - per * (o + 1)))
+        def _():
+            right2(b, t2ps).wait_recv()
+            t2ps[b] = t2[b] + t2pre[b]
+            right2(b, t2ps).start()
+
+        @pl.when((o == O - 1) & (il >= EARLY) & (il < nb2 - per))
+        def _():
+            left2(il, t2).start()
+
+        @pl.when((o < O - 1) & (il >= 0) & (il < per * o))
+        def _():
+            left2(il, t2ss).wait_recv()
+            t2ss[il] = t2[il] + t2suf[il]
+            left2(il, t2ss).start()
+
+    def own2():
+        for m in range(per):
+            b = o * per + m
+            tt[m] = t2[b]
+
+            @pl.when(o > 0)
+            def _():
+                right2(b, t2ps).wait_recv()
+                tt[m] += t2pre[b]
+
+            @pl.when(o < O - 1)
+            def _():
+                left2(b, t2ss).wait_recv()
+                tt[m] += t2suf[b]
+
+        for e in range(I - 1):
+            for n in range(per // I):
+                x2_copy(e, n).start()
+
+    def masked(g, p, pos0):
+        pos = pos0 + lax.broadcasted_iota(jnp.int32, (SUB, LANES), 0)
+        lane = lax.broadcasted_iota(jnp.int32, (SUB, LANES), 1)
+        return jnp.where(pos + jnp.where(lane < rank, 0, half) < lens[p], g, 0.0)
+
+    def gram(a, g):
+        return lax.dot_general(
+            a, g, (((0,), (0,)), ((), ())), precision=HIGHEST, preferred_element_type=jnp.float32
+        )
 
     def right_copy(b):
         return pltpu.make_async_remote_copy(
@@ -144,12 +251,8 @@
                 a += rx[e, t, 0]
                 g += rx[e, t, 1]
             own[t, 0] = a
-            tok0 = (t // spc) * ct
-            pos = tok0 % seq + (t % spc) * SUB + lax.broadcasted_iota(jnp.int32, (SUB, LANES), 0)
-            lane = lax.broadcasted_iota(jnp.int32, (SUB, LANES), 1)
-            pos = pos + jnp.where(lane < rank, 0, half)
-            length = lens[i * p_own + tok0 // seq]
-            own[t, 1] = jnp.where(pos < length, g, 0.0)
+            tok0 = i * rows_own + (t // spc) * ct
+            own[t, 1] = masked(g, tok0 // seq, tok0 % seq + (t % spc) * SUB)
 
         br = t - SKEW * o
 
@@ -185,16 +288,22 @@
             def _():
                 left_copy(bl).start()
 
+        if nc2:
+            @pl.when(t < nb)
+            def _():
+                relay2(t)
+
+            @pl.when(t == OWN2)
+            def _():
+                own2()
+
         b = t - SKEW * (O - 1)
 
         @pl.when(b >= 0)
         def _():
             def add(x):
-                p = ((b // spc) * ct) // seq
-                macc[p] += lax.dot_general(
-                    x, own[b, 1], (((0,), (0,)), ((), ())), precision=HIGHEST,
-                    preferred_element_type=jnp.float32,
-                )
+                p = (i * rows_own + (b // spc) * ct) // seq
+                macc[p] += gram(x, own[b, 1])
 
             @pl.when(o < O - 1)
             def _():
@@ -204,12 +313,25 @@
             def _():
                 add(psend[b])
 
+        if nc2:
+            @pl.when(t == nb + FIN)
+            def _():
+                for n in range(per // I):
+                    mine2 = i * (per // I) + n
+                    x = tt[mine2]
+                    for e in range(I - 1):
+                        x2_copy(e, n).wait_recv()
+                        x += rt[e, n]
+                    blk = o * per + mine2
+                    p = p_here - 1
+                    macc[p] += gram(x[0], masked(x[1], p, (blk // spc) * ct + (blk % spc) * SUB))
+
         return carry
 
     lax.fori_loop(0, nb + SKEW * (O - 1), third, 0)
 
     grows = gsend.shape[2]
-    for p in range(p_own):
+    for p in range(p_here):
         m = macc[p]
         g = m[:rank, :rank] + m[rank:, rank:]
         g2 = jnp.concatenate([g, g], axis=1)
@@ -235,10 +357,9 @@
     lane = lax.broadcasted_iota(jnp.int32, (1, LANES), 1)
     rows = []
     for p in range(p_here):
-        x, k = p // p_own, p % p_own
-        s = grecv[x, k]
-        for z in range(1, O):
-            s += grecv[z * I + x, k]
+        s = grecv[0, p]
+        for n in range(1, N):
+            s += grecv[n, p]
         flat = [
             jnp.where(lane < rank, s[2 * r : 2 * r + 1], s[2 * r + 1 : 2 * r + 2])
             for r in range(grows // 2)
@@ -280,6 +401,23 @@
         return carry
 
     lax.fori_loop(0, nb, drain, 0)
+
+    def drain2(b, carry):
+        @pl.when(o < b // per)
+        def _():
+            right2(b, t2ps).wait_send()
+
+        @pl.when(o > b // per)
+        def _():
+            left2(b, t2ss).wait_send()
+
+        return carry
+
+    if nc2:
+        lax.fori_loop(0, nb2, drain2, 0)
+        for e in range(I - 1):
+            for n in range(per // I):
+                x2_copy(e, n).wait_send()
     for d in range(1, N):
         d_copy(d).wait()
     total = drecv[0]
@@ -294,9 +432,12 @@
     N, Q = lax.axis_size("units"), lax.axis_size("prompts")
     I = inner
     O = N // I
-    p_own = p_here // I
-    rows_own = p_own * seq
     ct = min(1024, seq)
+    nb2 = seq // 2 // SUB
+    nc2 = seq // ct
+    if p_here < 2 or (p_here - 1) * seq % (I * ct) or nb2 % (O * I):
+        nc2 = nb2 = 0
+    rows_own = (p_here * seq - nc2 * ct) // I
     ncb = rows_own // ct
     spc = ct // 2 // SUB
     nb = ncb * spc
@@ -304,7 +445,8 @@
     grows = feats // rank
     nval = val_grads.shape[0] * Q
     cfg = dict(
-        N=N, I=I, O=O, Q=Q, ct=ct, ncb=ncb, nb=nb, spc=spc, seq=seq, p_here=p_here, p_own=p_own, rank=rank
+        N=N, I=I, O=O, Q=Q, ct=ct, ncb=ncb, nb=nb, spc=spc, seq=seq, p_here=p_here, rank=rank, nc2=nc2,
+        nb2=nb2,
     )
     f32 = jnp.float32
     dma = pltpu.SemaphoreType.DMA
@@ -329,17 +471,22 @@
             pltpu.VMEM((nb,) + block, f32),
             pltpu.VMEM((nb,) + block, f32),
             pltpu.VMEM((nb,) + block, f32),
-            pltpu.VMEM((p_own, LANES, LANES), f32),
-            pltpu.VMEM((N, p_own, grows, LANES), f32),
-            pltpu.VMEM((N, p_own, grows, LANES), f32),
+            pltpu.VMEM((p_here, LANES, LANES), f32),
+            pltpu.VMEM((N, p_here, grows, LANES), f32),
+            pltpu.VMEM((N, p_here, grows, LANES), f32),
             pltpu.VMEM((nval, feats), f32),
             pltpu.VMEM((drows, nval + LANES), f32),
             pltpu.VMEM((N, drows, nval + LANES), f32),
+            *[pltpu.VMEM((max(nb2, 1), 2) + block, f32)] * 5,
+            pltpu.VMEM((max(nb2 // O, 1), 2) + block, f32),
+            pltpu.VMEM((I - 1, max(nb2 // N, 1), 2) + block, f32),
             dma((2, 2)),
             dma((I - 1, nb)), dma((I - 1, nb)),
             dma((nb,)), dma((nb,)), dma((nb,)), dma((nb,)),
             dma((Q - 1,)), dma((Q - 1,)), dma,
             dma((N - 1,)), dma((N - 1,)), dma((N - 1,)), dma((N - 1,)),
+            *[dma((max(nb2, 1),))] * 4,
+            *[dma((I - 1, max(nb2 // N, 1)))] * 2,
         ],
         compiler_params=pltpu.CompilerParams(
             collective_id=0, has_side_effects=True, vmem_limit_bytes=60 * 1024 * 1024

time: 78.4 us -> 72.7 us (0.927)
  Pallas kernels: 76.9 us -> 71.2 us
    pallas_call x1, Pallas kernels: 76.9 us -> 71.2 us  [per_device(): pl.pallas_call(functools.partial(kernel, cfg), out_shape=jax.ShapeDtypeSt...]
where the time goes in v3:
time: 72.7 us; the launch traced here: 72.5 us
  Pallas kernels  71.2 us (98%)
  local copies, waits for them, and re-layouts  1.28 us (2%)
    pallas_call x1, Pallas kernels, per_device(): pl.pallas_call(functools.partial(kernel, cfg), out_shape=jax.ShapeDtypeSt...  71.2 us

profile of v3, /device:TPU:0, one launch (start us, length us, event | category | flops | bytes accessed | tf_op | source)
XLA Modules:
  0.0 72.5 jit_solution(1702070501051329947)
XLA Ops:
  0.0 71.2 %shard_map.64 = f32[4,256]{1,0:T(4,128)} custom-call(bf16[8192,1792]{1,0:T(8,128)(2,1)} %bitcast.4, bf16[8192,512]{1,0:T(8,128)(2,1)} %bitcast.5, bf16[64,1792]{1,0:T(8,128)(2,1)} %bitcast.6, bf16[64,512]{1,0:T(8,128)(2,1)} %bitcast.7, s32[4]{0:T(128)} %lens.1, f32[64,512]{1,0:T(8,128)} %val.1), custom_call_target="tpu_custom_call" | custom-call | tf_op jit(solution)/shard_map/pallas_call | solution.py:457
  71.2 1.3 %copy.8 = f32[4,256]{1,0:T(4,128)} copy(f32[4,256]{1,0:T(4,128)} %shard_map.64) | data formatting | bytes 8192
